TPU v7x, 256 devices: a whole 4x4x8 slice. The times are simulated.
256 devices in a mesh: tm: 8 (over x, core), strip: 32 (over z, y).
Axes of the slice: x: 4, y: 4, z: 8, core: 2. Of those that a mesh axis runs over, the one named last changes fastest.
Arguments:
- feature: bfloat16 [8, 64, 160, 384], P('tm', 'strip'), may hold values from -100 to 100
- frame_cache: bfloat16 [2, 64, 160, 384], P(None, 'strip'), may hold values from -6 to 6
- norm_gain: float32 [384], replicated, may hold values from 0.1 to 1.9
- conv_weight: bfloat16 [3, 3, 3, 384, 384], replicated, may hold values from -0.0625 to 0.0625
- conv_bias: float32 [384], replicated, may hold values from -3 to 3
- attn_gain: float32 [384], replicated, may hold values from 0.1 to 1.9
- qkv_weight: bfloat16 [384, 1152], replicated, may hold values from -2 to 2
- qkv_bias: float32 [1152], replicated, may hold values from -2 to 2
- out_weight: bfloat16 [384, 384], replicated, may hold values from -0.3125 to 0.3125
- out_bias: float32 [384], replicated, may hold values from -2 to 2
Outputs:
- mixed: bfloat16 [8, 64, 160, 384], P('tm', 'strip')
All inputs are finite; a program needn't handle non-finite values.
Results may differ from a plain program's by a relative error of at most 0.017.
Values may be sent and summed in bfloat16 or wider, within the bound.
No kernel may reach another device: no remote copies, remote signals or barrier semaphores. Data moves between devices by JAX's collectives and lax.ppermute only.
A program may use at most 128 MiB of HBM per device.

v0:
```python
import math
import jax
import jax.numpy as jnp
from jax import lax
from jax.sharding import PartitionSpec as P

epsilon = 1e-06


def shifted(x, axis, by):
    devices = lax.axis_size(axis)
    pairs = [(i, i + by) for i in range(devices) if 0 <= i + by < devices]
    return lax.ppermute(x, axis, pairs)


def padded_2(x, sides, width):
    for axis, dim in sides:
        devices, length = (lax.axis_size(axis), x.shape[dim])
        up = [(i, (i + 1) % devices) for i in range(devices - 1)]
        down = [(j, i) for i, j in up]
        last = lax.slice_in_dim(x, length - width, length, axis=dim)
        initial = lax.slice_in_dim(x, 0, width, axis=dim)
        before = lax.ppermute(last, axis, up)
        after = lax.ppermute(initial, axis, down)
        x = jnp.concatenate([before, x, after], axis=dim)
    return x


def normalize(values, gain):
    mean_square = jnp.mean(values * values, axis=-1, keepdims=True)
    return values * lax.rsqrt(mean_square + epsilon) * gain


def convolve(padded, conv_weight, height, width, channels):
    result = jnp.zeros((height * width, channels), jnp.float32)
    for frame_tap in range(3):
        for row_tap in range(3):
            row_band = padded[frame_tap, row_tap : row_tap + height]
            columns = jnp.concatenate(
                [row_band[:, col_tap : col_tap + width] for col_tap in range(3)], axis=-1
            )
            columns = columns.reshape(height * width, 3 * channels)
            result = result + jnp.dot(
                columns,
                conv_weight[frame_tap, row_tap].reshape(3 * channels, channels),
                preferred_element_type=jnp.float32,
            )
    return result


def local(
    feature,
    frame_cache,
    norm_gain,
    conv_weight,
    conv_bias,
    attn_gain,
    qkv_weight,
    qkv_bias,
    out_weight,
    out_bias,
):
    frames, height, width, channels = feature.shape
    values = feature.astype(jnp.float32)
    activated = jax.nn.silu(normalize(values, norm_gain)).astype(jnp.bfloat16)
    earlier = shifted(activated, "tm", 1)
    earliest = shifted(activated, "tm", 2)
    frame_index = lax.axis_index("tm")
    earlier = jnp.where(frame_index == 0, frame_cache[1:2], earlier)
    earliest = jnp.where(
        frame_index == 0, frame_cache[0:1], jnp.where(frame_index == 1, frame_cache[1:2], earliest)
    )
    stacked = jnp.concatenate([earliest, earlier, activated], axis=0)
    padded = padded_2(stacked, (("strip", 1),), 1)
    padded = jnp.pad(padded, ((0, 0), (0, 0), (1, 1), (0, 0)))
    branch = convolve(padded, conv_weight, height, width, channels)
    hidden = (values.reshape(-1, channels) + (branch + conv_bias)).astype(jnp.bfloat16)
    normed = normalize(hidden.astype(jnp.float32), attn_gain).astype(jnp.bfloat16)
    projected = (jnp.dot(normed, qkv_weight, preferred_element_type=jnp.float32) + qkv_bias).astype(
        jnp.bfloat16
    )
    queries = projected[:, :channels]
    score_scale = 1.0 / math.sqrt(channels)
    query_count = queries.shape[0]
    key_values = lax.all_gather(projected[:, channels:], "strip", axis=0, tiled=True)
    running_max = jnp.full((query_count,), -1e30, jnp.float32)
    scores = (
        jnp.einsum(
            "qc,kc->qk", queries, key_values[:, :channels], preferred_element_type=jnp.float32
        )
        * score_scale
    )
    highest = jnp.maximum(running_max, jnp.max(scores, axis=1))
    weights = jnp.exp(scores - highest[:, None])
    denominator = jnp.sum(weights, axis=1)
    numerator = jnp.dot(
        weights.astype(jnp.bfloat16), key_values[:, channels:], preferred_element_type=jnp.float32
    )
    attended = (numerator / denominator[:, None]).astype(jnp.bfloat16)
    result = (
        jnp.dot(attended, out_weight, preferred_element_type=jnp.float32)
        + out_bias
        + hidden.astype(jnp.float32)
    )
    return result.astype(jnp.bfloat16).reshape(frames, height, width, channels)


def solution(mesh):
    in_specs = (
        P("tm", "strip", None, None),
        P(None, "strip", None, None),
        P(),
        P(),
        P(),
        P(),
        P(),
        P(),
        P(),
        P(),
    )
    out_specs = P("tm", "strip", None, None)
    return jax.shard_map(local, mesh=mesh, in_specs=in_specs, out_specs=out_specs, check_vma=False)
```

profile of v0, /device:TPU:1, one launch (start us, length us, event | category | flops | bytes accessed | tf_op | source)
XLA Modules:
  0.0 220.8 jit_solution(4288578040709707474)
XLA Ops:
  6.5 0.0 copy-start
  6.5 0.0 all-gather.2.cloned.1.call-start
  6.5 1.2 multiply_reduce_fusion.1
  7.7 1.2 multiply_convert_fusion.1
  8.9 4.5 %collective-permute-start.1 = (bf16[1,2,160,384]{3,2,1,0:T(8,128)(2,1)S(1)}, bf16[1,2,160,384]{3,2,1,0:T(8,128)(2,1)S(1)}, u32[]{:S(2)}, u32[]{:S(2)}) collective-permute-start(bf16[1,2,160,384]{3,2,1,0:T(8,128)(2,1)S(1)} %multiply_convert_fusion.1), channel_id=1, source_target_pairs={{0,32},{32,64},{64,96},{96,128},{128,160},{160,192},{192,224},{1,3... | collective-permute-start | bytes 737288 | tf_op jit(solution)/shard_map/ppermute | solution.py:13
  13.4 3.1 %collective-permute-start = (bf16[1,2,160,384]{3,2,1,0:T(8,128)(2,1)S(1)}, bf16[1,2,160,384]{3,2,1,0:T(8,128)(2,1)S(1)}, u32[]{:S(2)}, u32[]{:S(2)}) collective-permute-start(bf16[1,2,160,384]{3,2,1,0:T(8,128)(2,1)S(1)} %multiply_convert_fusion.1), channel_id=1, source_target_pairs={{0,64},{32,96},{64,128},{96,160},{128,192},{160,224},{1,65},{33,97... | collective-permute-start | bytes 737288 | tf_op jit(solution)/shard_map/ppermute | solution.py:13
  16.6 0.0 collective-permute-done.1
  16.6 5.2 %collective-permute-done = bf16[1,2,160,384]{3,2,1,0:T(8,128)(2,1)S(1)} collective-permute-done((bf16[1,2,160,384]{3,2,1,0:T(8,128)(2,1)S(1)}, bf16[1,2,160,384]{3,2,1,0:T(8,128)(2,1)S(1)}, u32[]{:S(2)}, u32[]{:S(2)}) %collective-permute-start) | collective-permute-done | bytes 245792 | tf_op jit(solution)/shard_map/ppermute | solution.py:13
  21.8 1.1 select_select_fusion
  22.9 0.1 pad_maximum_fusion
  23.1 0.1 fusion.39
  23.1 3.2 %collective-permute-start.2 = (bf16[3,1,160,384]{3,2,1,0:T(8,128)(2,1)S(1)}, bf16[3,1,160,384]{3,2,1,0:T(8,128)(2,1)S(1)}, u32[]{:S(2)}, u32[]{:S(2)}) collective-permute-start(bf16[3,1,160,384]{3,2,1,0:T(8,128)(2,1)S(1)} %get-tuple-element.23), channel_id=1, source_target_pairs={{0,1},{1,2},{2,3},{3,4},{4,5},{5,6},{6,7},{7,8},{8,9},{9,10},{10,1... | collective-permute-start | bytes 1105928 | tf_op jit(solution)/shard_map/ppermute | solution.py:23
  26.4 1.3 collective-permute-start.3
  27.7 3.9 %fusion.38 = (bf16[1,1,3,384,384]{4,3,2,1,0:T(8,128)(2,1)S(1)}, bf16[1,1,3,384,384]{4,3,2,1,0:T(8,128)(2,1)S(1)}, bf16[1,1,3,384,384]{4,3,2,1,0:T(8,128)(2,1)S(1...) fusion(bf16[3,3,3,384,384]{4,3,2,1,0:T(8,128)(2,1)} %param.13), kind=kLoop, calls=%fused_computation.69 | loop fusion | bytes 15925248 | tf_op jit(solution)/shard_map/slice | solution.py:45
  31.6 2.8 %collective-permute-done.2 = bf16[3,1,160,384]{3,2,1,0:T(8,128)(2,1)S(1)} collective-permute-done((bf16[3,1,160,384]{3,2,1,0:T(8,128)(2,1)S(1)}, bf16[3,1,160,384]{3,2,1,0:T(8,128)(2,1)S(1)}, u32[]{:S(2)}, u32[]{:S(2)}) %collective-permute-start.2) | collective-permute-done | bytes 368672 | tf_op jit(solution)/shard_map/ppermute | solution.py:23
  34.4 3.8 %collective-permute-done.3 = bf16[3,1,160,384]{3,2,1,0:T(8,128)(2,1)S(1)} collective-permute-done((bf16[3,1,160,384]{3,2,1,0:T(8,128)(2,1)S(1)}, bf16[3,1,160,384]{3,2,1,0:T(8,128)(2,1)S(1)}, u32[]{:S(2)}, u32[]{:S(2)}) %collective-permute-start.3) | collective-permute-done | bytes 368672 | tf_op jit(solution)/shard_map/ppermute | solution.py:24
  38.2 0.4 select_maximum_fusion
  38.7 0.2 slice_bitcast_fusion
  38.9 0.1 fusion.48
  39.0 0.3 fusion.40
  39.3 0.3 fusion.42
  39.6 0.3 fusion.44
  39.9 0.3 fusion.46
  40.1 0.1 pad_maximum_fusion.1
  40.2 0.6 fusion.50
  40.8 0.1 pad_maximum_fusion.9
  40.9 0.1 pad_maximum_fusion.8
  40.9 0.1 pad_maximum_fusion.7
  41.0 0.1 pad_maximum_fusion.6
  41.1 0.1 pad_maximum_fusion.5
  41.2 0.1 pad_maximum_fusion.4
  41.2 0.1 pad_maximum_fusion.3
  41.3 0.1 pad_maximum_fusion.2
  41.4 0.6 convolution_add_fusion.8
  42.0 0.6 convolution_add_fusion.7
  42.6 0.6 convolution_add_fusion.6
  43.2 0.6 convolution_add_fusion.5
  43.8 0.6 convolution_add_fusion.4
  44.4 0.6 convolution_add_fusion.3
  45.0 0.0 copy-start.3
  45.0 0.0 copy-start.5
  45.0 0.6 convolution_add_fusion.2
  45.6 0.0 copy-start.4
  45.6 0.0 copy-start.6
  45.6 0.3 copy-done.3
  45.9 0.0 copy-done.5
  45.9 0.7 multiply_reduce_fusion
  46.6 0.0 copy-done
  46.6 0.0 copy-done.4
  46.6 0.0 copy-done.6
  46.7 0.6 fusion.8
  47.3 0.9 slice.252
  48.1 0.0 all-gather.2.cloned.1.call-update
  48.2 141.0 %all-gather.2.cloned.1.call-done = bf16[10240,768]{1,0:T(8,128)(2,1)} async-done(((bf16[320,768]{1,0:T(8,128)(2,1)}), bf16[10240,768]{1,0:T(8,128)(2,1)}) %all-gather.2.cloned.1.call-update) | async-done | bytes 15728656 | tf_op jit(solution)/shard_map/all_gather | solution.py:85
  189.1 6.3 %fusion.49 = (f32[320]{0:T(512)S(1)}, f32[320,10240]{1,0:T(8,128)S(1)}) fusion(bf16[10240,768]{1,0:T(8,128)(2,1)} %all-gather.2.cloned.1.call-done, bf16[320,1152]{1,0:T(8,128)(2,1)S(1)} %fusion.8), kind=kOutput, calls=%fused_computation.80 | convolution fusion | flops 2523135744 | bytes 21218560 | tf_op jit(solution)/shard_map/qc,kc->qk/dot_general | solution.py:88
  195.5 0.0 copy-start.2
  195.5 4.7 %copy-done.2 = f32[320,10240]{1,0:T(8,128)} copy-done((f32[320,10240]{1,0:T(8,128)}, f32[320,10240]{1,0:T(8,128)S(1)}, u32[]{:S(2)}) %copy-start.2) | copy-done | bytes 13107224
  200.2 0.0 copy-start.7
  200.2 2.1 fusion
  202.3 0.0 copy-done.7
  202.3 0.0 copy-done.8
  202.3 0.0 copy-start.1
  202.3 11.6 %fusion.17 = bf16[320,384]{1,0:T(8,128)(2,1)} fusion(f32[320,384]{1,0:T(8,128)S(1)} %get-tuple-element.55, bf16[384,384]{1,0:T(8,128)(2,1)S(1)} %copy-done.7, bf16[10240,768]{1,0:T(8,128)(2,1)} %all-gather.2.cloned.1.call-done, f32[320,10240]{1,0:T(8,128)} %copy-done.2, f32[320]{0:T(512)S(1)} %broadcast_maximum_fusion, f32[384]{0:T(512)S(1)} %copy-done.8, ...), kind=kOutput, calls=%fused_computation.32 | convolution fusion | flops 2618122240 | bytes 22007808 | tf_op jit(solution)/shard_map/dot_general | solution.py:101
  214.0 0.0 copy-done.1
  (4 shorter events, 0.0 us)
Async XLA Ops:
  6.5 40.1 %copy-start = (bf16[384,1152]{1,0:T(8,128)(2,1)S(1)}, bf16[384,1152]{1,0:T(8,128)(2,1)}, u32[]{:S(2)}) copy-start(bf16[384,1152]{1,0:T(8,128)(2,1)} %param.16) | copy-start | bytes 2654212
  6.5 182.6 %all-gather.2.cloned.1.call-start = ((), (), s32[]{:S(2)}) async-start(), calls=%async_computation | async-start | bytes 16220160 | tf_op jit(solution)/shard_map/all_gather | solution.py:85
  8.9 7.7 %collective-permute-start.1 = (bf16[1,2,160,384]{3,2,1,0:T(8,128)(2,1)S(1)}, bf16[1,2,160,384]{3,2,1,0:T(8,128)(2,1)S(1)}, u32[]{:S(2)}, u32[]{:S(2)}) collective-permute-start(bf16[1,2,160,384]{3,2,1,0:T(8,128)(2,1)S(1)} %multiply_convert_fusion.1), channel_id=1, source_target_pairs={{0,32},{32,64},{64,96},{96,128},{128,160},{160,192},{192,224},{1,3... | collective-permute-start | bytes 737288 | tf_op jit(solution)/shard_map/ppermute | solution.py:13
  13.4 8.4 %collective-permute-start = (bf16[1,2,160,384]{3,2,1,0:T(8,128)(2,1)S(1)}, bf16[1,2,160,384]{3,2,1,0:T(8,128)(2,1)S(1)}, u32[]{:S(2)}, u32[]{:S(2)}) collective-permute-start(bf16[1,2,160,384]{3,2,1,0:T(8,128)(2,1)S(1)} %multiply_convert_fusion.1), channel_id=1, source_target_pairs={{0,64},{32,96},{64,128},{96,160},{128,192},{160,224},{1,65},{33,97... | collective-permute-start | bytes 737288 | tf_op jit(solution)/shard_map/ppermute | solution.py:13
  23.1 11.3 %collective-permute-start.2 = (bf16[3,1,160,384]{3,2,1,0:T(8,128)(2,1)S(1)}, bf16[3,1,160,384]{3,2,1,0:T(8,128)(2,1)S(1)}, u32[]{:S(2)}, u32[]{:S(2)}) collective-permute-start(bf16[3,1,160,384]{3,2,1,0:T(8,128)(2,1)S(1)} %get-tuple-element.23), channel_id=1, source_target_pairs={{0,1},{1,2},{2,3},{3,4},{4,5},{5,6},{6,7},{7,8},{8,9},{9,10},{10,1... | collective-permute-start | bytes 1105928 | tf_op jit(solution)/shard_map/ppermute | solution.py:23
  26.4 11.9 %collective-permute-start.3 = (bf16[3,1,160,384]{3,2,1,0:T(8,128)(2,1)S(1)}, bf16[3,1,160,384]{3,2,1,0:T(8,128)(2,1)S(1)}, u32[]{:S(2)}, u32[]{:S(2)}) collective-permute-start(bf16[3,1,160,384]{3,2,1,0:T(8,128)(2,1)S(1)} %get-tuple-element.24), channel_id=1, source_target_pairs={{1,0},{2,1},{3,2},{4,3},{5,4},{6,5},{7,6},{8,7},{9,8},{10,9},{11,1... | collective-permute-start | bytes 1105928 | tf_op jit(solution)/shard_map/ppermute | solution.py:24
  45.0 0.9 copy-start.3
  45.0 0.9 copy-start.5
  45.6 1.1 copy-start.4
  45.6 1.1 copy-start.6
  195.5 4.7 %copy-start.2 = (f32[320,10240]{1,0:T(8,128)}, f32[320,10240]{1,0:T(8,128)S(1)}, u32[]{:S(2)}) copy-start(f32[320,10240]{1,0:T(8,128)S(1)} %get-tuple-element.57) | copy-start | bytes 39321604
  200.2 2.1 copy-start.7
  200.2 2.1 copy-start.8
  202.3 11.6 %copy-start.1 = (bf16[384,1152]{1,0:T(8,128)(2,1)S(1)}, bf16[384,1152]{1,0:T(8,128)(2,1)}, u32[]{:S(2)}) copy-start(bf16[384,1152]{1,0:T(8,128)(2,1)} %param.16) | copy-start | bytes 2654212
Sparse Core Ops, SparseCore 0:
  48.3 140.8 all-gather.1
where the time goes:
time: 221 us
  waiting for transfers between devices  153 us (69%)
  matrix products  24 us (11%)
  between operations  13.8 us (6%)
  starting transfers between devices  12.2 us (6%)
  local copies, waits for them, and re-layouts  11.4 us (5%)
  other arithmetic  6.73 us (3%)
    all_gather x1, waiting for transfers between devices, local(): lax.all_gather(projected[:, channels:], 'strip', axis=0, tiled=True)  141 us
    dot_general x1, matrix products, local(): jnp.dot(attended, out_weight, preferred_element_type=jnp.float32) + out_bias  11.6 us
    ppermute x2, starting transfers between devices, shifted(): return lax.ppermute(x, axis, pairs)  7.64 us
    dot_general x1, matrix products, local(): jnp.einsum('qc,kc->qk', queries, key_values[:, :channels], preferred_elem...  6.31 us
    dot_general x9, matrix products, convolve(): jnp.dot(columns, conv_weight[frame_tap, row_tap].reshape(3 * channels, ch...  5.41 us
    ppermute x2, waiting for transfers between devices, shifted(): return lax.ppermute(x, axis, pairs)  5.23 us
    unnamed x18, local copies, waits for them, and re-layouts  5.06 us
  transfers between devices with their start and end apart: 5, of which 4 were waited for; matrix products, arithmetic and copies ran while one was open for 2% of the time, Pallas kernels for 0%

commit v1 on v0

--- a/solution.py
+++ b/solution.py
@@ -82,7 +82,12 @@
     queries = projected[:, :channels]
     score_scale = 1.0 / math.sqrt(channels)
     query_count = queries.shape[0]
-    key_values = lax.all_gather(projected[:, channels:], "strip", axis=0, tiled=True)
+    key_values = jnp.concatenate(
+        lax.all_to_all(
+            jnp.stack([projected[:, channels:]] * lax.axis_size("strip")), "strip", 0, 0
+        ),
+        axis=0,
+    )
     running_max = jnp.full((query_count,), -1e30, jnp.float32)
     scores = (
         jnp.einsum(

time: 221 us -> 423 us (1.91)
  blocking collectives: 0 us -> 353 us
  waiting for transfers between devices: 153 us -> 11.8 us
  between operations: 13.8 us -> 0.39 us
    all_to_all x0 -> x1, blocking collectives: none -> 353 us  [local(): lax.all_to_all(jnp.stack([projected[:, channels:]] * lax.axis_size('strip...]
    all_gather x1 -> x0, waiting for transfers between devices: 141 us -> none  [local(): lax.all_gather(projected[:, channels:], 'strip', axis=0, tiled=True)]
  transfers between devices with their start and end apart: 5 -> 4, of which waited for: 4 -> 3; matrix products, arithmetic and copies ran while one was open for 2% -> 1% of each run, Pallas kernels for 0% -> 0%
where the time goes in v1:
time: 423 us; the launch traced here: 421 us
  blocking collectives  353 us (83%)
  matrix products  23.8 us (6%)
  local copies, waits for them, and re-layouts  12.4 us (3%)
  starting transfers between devices  12.2 us (3%)
  waiting for transfers between devices  11.8 us (3%)
  other arithmetic  6.73 us (2%)
    all_to_all x1, blocking collectives, local(): lax.all_to_all(jnp.stack([projected[:, channels:]] * lax.axis_size('strip...  353 us
    dot_general x1, matrix products, local(): jnp.dot(attended, out_weight, preferred_element_type=jnp.float32) + out_bias  11.6 us
  transfers between devices with their start and end apart: 4, of which 3 were waited for; matrix products, arithmetic and copies ran while one was open for 1% of the time, Pallas kernels for 0%

profile of v1, /device:TPU:1, one launch (start us, length us, event | category | flops | bytes accessed | tf_op | source)
XLA Modules:
  0.0 420.5 jit_solution(18106797968045898258)
XLA Ops:
  0.0 0.0 copy-start
  0.0 1.2 multiply_reduce_fusion.1
  1.2 1.2 multiply_convert_fusion.1
  2.4 4.5 %collective-permute-start.1 = (bf16[1,2,160,384]{3,2,1,0:T(8,128)(2,1)S(1)}, bf16[1,2,160,384]{3,2,1,0:T(8,128)(2,1)S(1)}, u32[]{:S(2)}, u32[]{:S(2)}) collective-permute-start(bf16[1,2,160,384]{3,2,1,0:T(8,128)(2,1)S(1)} %multiply_convert_fusion.1), channel_id=1, source_target_pairs={{0,32},{32,64},{64,96},{96,128},{128,160},{160,192},{192,224},{1,3... | collective-permute-start | bytes 737288 | tf_op jit(solution)/shard_map/ppermute | solution.py:13
  6.9 3.1 collective-permute-start
  10.0 0.0 collective-permute-done.1
  10.1 5.2 %collective-permute-done = bf16[1,2,160,384]{3,2,1,0:T(8,128)(2,1)S(1)} collective-permute-done((bf16[1,2,160,384]{3,2,1,0:T(8,128)(2,1)S(1)}, bf16[1,2,160,384]{3,2,1,0:T(8,128)(2,1)S(1)}, u32[]{:S(2)}, u32[]{:S(2)}) %collective-permute-start) | collective-permute-done | bytes 245792 | tf_op jit(solution)/shard_map/ppermute | solution.py:13
  15.3 1.1 select_select_fusion
  16.4 0.1 pad_maximum_fusion
  16.5 0.1 fusion.39
  16.6 3.2 collective-permute-start.2
  19.8 1.3 collective-permute-start.3
  21.1 3.9 fusion.38
  25.1 2.8 collective-permute-done.2
  27.9 3.8 collective-permute-done.3
  31.7 0.4 select_maximum_fusion
  32.1 0.2 slice_bitcast_fusion
  32.3 0.1 fusion.48
  32.5 0.3 fusion.40
  32.8 0.3 fusion.42
  33.0 0.3 fusion.44
  33.3 0.3 fusion.46
  33.6 0.1 pad_maximum_fusion.1
  33.7 0.6 fusion.50
  34.3 0.1 pad_maximum_fusion.9
  34.3 0.1 pad_maximum_fusion.8
  34.4 0.1 pad_maximum_fusion.7
  34.5 0.1 pad_maximum_fusion.6
  34.6 0.1 pad_maximum_fusion.5
  34.6 0.1 pad_maximum_fusion.4
  34.7 0.1 pad_maximum_fusion.3
  34.8 0.1 pad_maximum_fusion.2
  34.9 0.6 convolution_add_fusion.8
  35.4 0.6 convolution_add_fusion.7
  36.0 0.6 convolution_add_fusion.6
  36.6 0.6 convolution_add_fusion.5
  37.2 0.6 convolution_add_fusion.4
  37.8 0.6 convolution_add_fusion.3
  38.4 0.0 copy-start.3
  38.4 0.0 copy-start.5
  38.4 0.6 convolution_add_fusion.2
  39.0 0.0 copy-start.4
  39.1 0.0 copy-start.6
  39.1 0.3 copy-done.3
  39.4 0.0 copy-done.5
  39.4 0.7 multiply_reduce_fusion
  40.1 0.0 copy-done
  40.1 0.0 copy-done.4
  40.1 0.0 copy-done.6
  40.1 0.6 fusion.8
  40.8 1.8 stack.2
  42.6 353.2 %all_to_all.5 = bf16[32,320,768]{2,1,0:T(8,128)(2,1)} all-to-all(bf16[32,320,768]{2,1,0:T(8,128)(2,1)S(1)} %stack.2), channel_id=1, replica_groups=mesh['tm'=8,'strip'=32] {'strip'}, dimensions={0} | all-to-all | bytes 31457280 | tf_op jit(solution)/shard_map/all_to_all | solution.py:86
  395.9 6.2 %fusion.49 = (f32[320]{0:T(512)S(1)}, f32[320,10240]{1,0:T(8,128)S(1)}) fusion(bf16[10240,768]{1,0:T(8,128)(2,1)} %bitcast.60, bf16[320,1152]{1,0:T(8,128)(2,1)S(1)} %fusion.8), kind=kOutput, calls=%fused_computation.80 | convolution fusion | flops 2523135744 | bytes 21218560 | tf_op jit(solution)/shard_map/qc,kc->qk/dot_general | solution.py:93
  402.0 0.0 copy-start.2
  402.1 4.7 %copy-done.2 = f32[320,10240]{1,0:T(8,128)} copy-done((f32[320,10240]{1,0:T(8,128)}, f32[320,10240]{1,0:T(8,128)S(1)}, u32[]{:S(2)}) %copy-start.2) | copy-done | bytes 13107224
  406.8 0.0 copy-start.7
  406.8 0.0 copy-start.8
  406.8 2.1 fusion
  408.9 0.0 copy-done.7
  408.9 0.0 copy-done.8
  408.9 0.0 copy-start.1
  408.9 11.6 %fusion.17 = bf16[320,384]{1,0:T(8,128)(2,1)} fusion(f32[320,384]{1,0:T(8,128)S(1)} %get-tuple-element.55, bf16[384,384]{1,0:T(8,128)(2,1)S(1)} %copy-done.7, bf16[10240,768]{1,0:T(8,128)(2,1)} %bitcast.61, f32[320,10240]{1,0:T(8,128)} %copy-done.2, f32[320]{0:T(512)S(1)} %broadcast_maximum_fusion, f32[384]{0:T(512)S(1)} %copy-done.8, f32[320]{0:T(512)S(1)} %fusion), kind=kOutput, calls=%fused_computation.32 | convolution fusion | flops 2618122240 | bytes 22007808 | tf_op jit(solution)/shard_map/dot_general | solution.py:106
  420.5 0.0 copy-done.1
  (4 shorter events, 0.1 us)
Async XLA Ops:
  0.0 40.1 %copy-start = (bf16[384,1152]{1,0:T(8,128)(2,1)S(1)}, bf16[384,1152]{1,0:T(8,128)(2,1)}, u32[]{:S(2)}) copy-start(bf16[384,1152]{1,0:T(8,128)(2,1)} %param.16) | copy-start | bytes 2654212
  2.4 7.7 %collective-permute-start.1 = (bf16[1,2,160,384]{3,2,1,0:T(8,128)(2,1)S(1)}, bf16[1,2,160,384]{3,2,1,0:T(8,128)(2,1)S(1)}, u32[]{:S(2)}, u32[]{:S(2)}) collective-permute-start(bf16[1,2,160,384]{3,2,1,0:T(8,128)(2,1)S(1)} %multiply_convert_fusion.1), channel_id=1, source_target_pairs={{0,32},{32,64},{64,96},{96,128},{128,160},{160,192},{192,224},{1,3... | collective-permute-start | bytes 737288 | tf_op jit(solution)/shard_map/ppermute | solution.py:13
  6.9 8.4 %collective-permute-start = (bf16[1,2,160,384]{3,2,1,0:T(8,128)(2,1)S(1)}, bf16[1,2,160,384]{3,2,1,0:T(8,128)(2,1)S(1)}, u32[]{:S(2)}, u32[]{:S(2)}) collective-permute-start(bf16[1,2,160,384]{3,2,1,0:T(8,128)(2,1)S(1)} %multiply_convert_fusion.1), channel_id=1, source_target_pairs={{0,64},{32,96},{64,128},{96,160},{128,192},{160,224},{1,65},{33,97... | collective-permute-start | bytes 737288 | tf_op jit(solution)/shard_map/ppermute | solution.py:13
  16.6 11.3 %collective-permute-start.2 = (bf16[3,1,160,384]{3,2,1,0:T(8,128)(2,1)S(1)}, bf16[3,1,160,384]{3,2,1,0:T(8,128)(2,1)S(1)}, u32[]{:S(2)}, u32[]{:S(2)}) collective-permute-start(bf16[3,1,160,384]{3,2,1,0:T(8,128)(2,1)S(1)} %get-tuple-element.23), channel_id=1, source_target_pairs={{0,1},{1,2},{2,3},{3,4},{4,5},{5,6},{6,7},{7,8},{8,9},{9,10},{10,1... | collective-permute-start | bytes 1105928 | tf_op jit(solution)/shard_map/ppermute | solution.py:23
  19.8 11.9 %collective-permute-start.3 = (bf16[3,1,160,384]{3,2,1,0:T(8,128)(2,1)S(1)}, bf16[3,1,160,384]{3,2,1,0:T(8,128)(2,1)S(1)}, u32[]{:S(2)}, u32[]{:S(2)}) collective-permute-start(bf16[3,1,160,384]{3,2,1,0:T(8,128)(2,1)S(1)} %get-tuple-element.24), channel_id=1, source_target_pairs={{1,0},{2,1},{3,2},{4,3},{5,4},{6,5},{7,6},{8,7},{9,8},{10,9},{11,1... | collective-permute-start | bytes 1105928 | tf_op jit(solution)/shard_map/ppermute | solution.py:24
  38.4 0.9 copy-start.3
  38.4 0.9 copy-start.5
  39.0 1.1 copy-start.4
  39.1 1.1 copy-start.6
  402.0 4.7 %copy-start.2 = (f32[320,10240]{1,0:T(8,128)}, f32[320,10240]{1,0:T(8,128)S(1)}, u32[]{:S(2)}) copy-start(f32[320,10240]{1,0:T(8,128)S(1)} %get-tuple-element.57) | copy-start | bytes 39321604
  406.8 2.1 copy-start.7
  406.8 2.1 copy-start.8
  408.9 11.6 %copy-start.1 = (bf16[384,1152]{1,0:T(8,128)(2,1)S(1)}, bf16[384,1152]{1,0:T(8,128)(2,1)}, u32[]{:S(2)}) copy-start(bf16[384,1152]{1,0:T(8,128)(2,1)} %param.16) | copy-start | bytes 2654212
